TPU v7x, 128 devices: a whole 4x4x4 slice. The times are simulated.
128 devices in a mesh: grp: 8 (over y, core), tok: 16 (over z, x).
Axes of the slice: x: 4, y: 4, z: 4, core: 2. Of those that a mesh axis runs over, the one named last changes fastest.
Arguments:
- pre_q: bfloat16 [8192, 4096], P(('grp', 'tok')), may hold values from -64 to 64
- pre_kv: bfloat16 [8192, 2048], P(('grp', 'tok')), may hold values from -8 to 8
- pre_segment: int32 [8, 1024], P('grp'), may hold values from 0 to 3, never falling along the last dimension, each value on 1 to 512 neighbouring positions
- dec_q: bfloat16 [128, 4096], P(('grp', 'tok')), may hold values from -64 to 64
- cache: bfloat16 [128, 512, 2048], P(('grp', 'tok')), may hold values from -8 to 8
- cache_len: int32 [128], P(('grp', 'tok')), may hold values from 1 to 512, 32768 in all
- slot_request: int32 [128], replicated, may hold values from 0 to 127, each once
- resid: bfloat16 [8320, 4096], P('grp', 'tok'), may hold values from -64 to 64
- wo: bfloat16 [4096, 4096], P(None, 'tok'), may hold values from -0.5 to 0.5
- tenant: int32 [8, 1040], P('grp'), may hold values from 0 to 3, never falling along the last dimension, each value on 1 to 520 neighbouring positions
- norm_gain: float32 [4, 4096], replicated, may hold values from 0.25 to 1.75
- w_gate: bfloat16 [4096, 12288], P(None, 'tok'), may hold values from -0.09375 to 0.09375
- w_up: bfloat16 [4096, 12288], P(None, 'tok'), may hold values from -0.09375 to 0.09375
- w_down: bfloat16 [12288, 4096], P('tok'), may hold values from -0.0546875 to 0.0546875
Outputs:
- out: bfloat16 [8320, 4096], P('grp', 'tok')
All inputs are finite; a program needn't handle non-finite values. No bound on the sum of `cache_len` on one device may be relied on, other than what follows from the above.
Results may differ from a plain program's by a relative error of at most 0.011.
Values may be sent and summed in bfloat16 or wider, within the bound.
A program may use at most 128 MiB of HBM per device.

v0:
```python
import math
import jax
import jax.numpy as jnp
from jax import lax
from jax.sharding import PartitionSpec as P

D = 4096
H = 32
KVH = 8
HD = 128
epsilon = 1e-05


def laid_out(blocks, dim):
    dims = list(blocks.shape[1:])
    dims[dim] *= blocks.shape[0]
    return jnp.moveaxis(blocks, 0, dim).reshape(dims)


def piecewise(x, axis, dim, apply, out_dim):
    size, span = (lax.axis_size(axis), x.shape[dim])
    count = 2 if span % 2 == 0 else 1
    gathered, length = ([], span // count)
    for k in range(count):
        share = lax.slice_in_dim(x, k * length, (k + 1) * length, axis=dim)
        starts = jnp.arange(size) * span + k * length
        gathered.append(jax.vmap(apply)(lax.all_gather(share, axis), starts))
    return laid_out(jnp.concatenate(gathered, axis=out_dim + 1), out_dim)


def copy_for_each(x, axis):
    copies = jnp.broadcast_to(x, (lax.axis_size(axis), *x.shape))
    return lax.all_to_all(copies, axis, split_axis=0, concat_axis=0, tiled=True)


def over_copies(x, axis):
    return copy_for_each(x, axis).sum(axis=0)


def shards(
    pre_q,
    pre_kv,
    pre_segment,
    dec_q,
    cache,
    cache_len,
    slot_request,
    resid,
    wo,
    tenant,
    norm_gain,
    w_gate,
    w_up,
    w_down,
):
    group = H // KVH
    width = KVH * HD
    tok_index = lax.axis_index("tok")
    local_rows = pre_q.shape[0]
    segment = pre_segment[0]
    query_pos = tok_index * local_rows + jnp.arange(local_rows)
    query_seg = lax.dynamic_slice_in_dim(segment, tok_index * local_rows, local_rows)
    queries = pre_q.reshape(local_rows, KVH, group, HD)
    piece = lax.all_gather(pre_kv, "tok", axis=0, tiled=True)
    running = jnp.full((KVH, group, local_rows), -jnp.inf, jnp.float32)
    totals = jnp.zeros((KVH, group, local_rows), jnp.float32)
    summed = jnp.zeros((KVH, group, local_rows, HD), jnp.float32)
    count = piece.shape[0]
    keys = piece[:, :width].reshape(count, KVH, HD)
    values = piece[:, width:].reshape(count, KVH, HD)
    key_pos = jnp.arange(count)
    allowed = (key_pos[None, :] <= query_pos[:, None]) & (segment[None, :] == query_seg[:, None])
    scores = jnp.einsum(
        "qkgd,nkd->kgqn", queries, keys, preferred_element_type=jnp.float32
    ) / math.sqrt(HD)
    scores = jnp.where(allowed, scores, -jnp.inf)
    highest = jnp.max(scores, axis=-1)
    anchor = jnp.where(jnp.isfinite(highest), highest, 0.0)
    weights = jnp.exp(scores - anchor[..., None]).astype(jnp.bfloat16)
    factor = jnp.exp(running - anchor)
    totals = totals * factor + jnp.sum(weights.astype(jnp.float32), axis=-1)
    summed = summed * factor[..., None] + jnp.einsum(
        "kgqn,nkd->kgqd", weights, values, preferred_element_type=jnp.float32
    )
    running, totals, summed = (highest, totals, summed)
    prefill_out = (
        (summed / totals[..., None])
        .transpose(2, 0, 1, 3)
        .reshape(local_rows, D)
        .astype(jnp.bfloat16)
    )
    all_queries = lax.all_gather(dec_q, ("grp", "tok"), axis=0, tiled=True)
    slot = lax.axis_index(("grp", "tok"))
    request = slot_request[slot]
    query_row = lax.dynamic_slice_in_dim(all_queries, request, 1, 0).reshape(KVH, group, HD)
    positions = cache.shape[1]
    entries = cache[0].reshape(positions, 2, KVH, HD)
    slot_scores = jnp.einsum(
        "kgd,pkd->kgp", query_row, entries[:, 0], preferred_element_type=jnp.float32
    ) / math.sqrt(HD)
    visible = jnp.arange(positions) < cache_len[0]
    slot_scores = jnp.where(visible, slot_scores, -jnp.inf)
    slot_top = jnp.max(slot_scores, axis=-1, keepdims=True)
    slot_weights = jnp.exp(slot_scores - slot_top).astype(jnp.bfloat16)
    slot_total = jnp.sum(slot_weights.astype(jnp.float32), axis=-1)
    slot_mixed = jnp.einsum(
        "kgp,pkd->kgd", slot_weights, entries[:, 1], preferred_element_type=jnp.float32
    )
    decode_out = (slot_mixed / slot_total[..., None]).reshape(1, D).astype(jnp.bfloat16)
    attended = jnp.concatenate([prefill_out, decode_out], axis=0)

    def project(piece, start):
        return jnp.dot(piece, wo, preferred_element_type=jnp.float32)

    projected = piecewise(attended, "tok", 0, project, 0)
    mixed_in = (resid.astype(jnp.float32) + projected).astype(jnp.bfloat16)
    col_count = mixed_in.shape[1]
    owners = tenant[0]
    one_hot = (owners[:, None] == jnp.arange(norm_gain.shape[0])[None, :]).astype(jnp.float32)
    wide_cols = mixed_in.astype(jnp.float32)
    partial_sq = jnp.sum(wide_cols * wide_cols, axis=-1)
    square_sum = over_copies(partial_sq, "tok")
    local_gain = lax.dynamic_slice_in_dim(norm_gain, tok_index * col_count, col_count, 1)
    gains = jnp.dot(one_hot, local_gain, precision=lax.Precision.HIGHEST)
    normed_part = (wide_cols * lax.rsqrt(square_sum / D + epsilon)[:, None] * gains).astype(
        jnp.bfloat16
    )
    piece = lax.all_gather(normed_part, "tok", axis=1, tiled=True)
    gate_part = jnp.dot(piece, w_gate, preferred_element_type=jnp.float32)
    lift_part = jnp.dot(piece, w_up, preferred_element_type=jnp.float32)
    hidden = (jax.nn.silu(gate_part) * lift_part).astype(jnp.bfloat16)
    summed_cols = lax.psum_scatter(
        lax.dot_general(
            w_down, hidden, (((0,), (1,)), ((), ())), preferred_element_type=jnp.float32
        ).astype(jnp.bfloat16),
        "tok",
        scatter_dimension=0,
        tiled=True,
    ).astype(jnp.float32)
    result = mixed_in.astype(jnp.float32) + summed_cols.T
    return result.astype(jnp.bfloat16)


def solution(mesh):
    in_specs = (
        P(("grp", "tok"), None),
        P(("grp", "tok"), None),
        P("grp", None),
        P(("grp", "tok"), None),
        P(("grp", "tok"), None, None),
        P(("grp", "tok")),
        P(),
        P("grp", "tok"),
        P(None, "tok"),
        P("grp", None),
        P(),
        P(None, "tok"),
        P(None, "tok"),
        P("tok", None),
    )
    out_specs = P("grp", "tok")
    return jax.shard_map(shards, mesh=mesh, in_specs=in_specs, out_specs=out_specs, check_vma=False)
```

profile of v0, /device:TPU:1, one launch (start us, length us, event | category | flops | bytes accessed | tf_op | source)
XLA Modules:
  0.0 468.5 jit_solution(10560985726428544450)
XLA Ops:
  6.5 0.0 copy-start
  6.5 0.0 copy-start.4
  6.5 0.0 all-gather.12.cloned.1.call-start
  6.5 0.7 all-gather.12.cloned.1.call-update
  7.3 0.0 all-gather.8.cloned.1.call-start
  7.3 0.7 all-gather.8.cloned.1.call-update
  8.0 0.0 all-gather.14.cloned.1.call-start
  8.1 1.2 dynamic_slice.13
  11.3 1.4 reshape.65
  12.7 4.0 copy.48
  17.3 0.0 copy-done.4
  17.3 0.1 fusion.29
  17.4 0.1 fusion.22
  17.5 61.7 %all-gather.12.cloned.1.call-done = bf16[128,1,4096]{2,1,0:T(2,128)(2,1)} async-done(((bf16[1,1,4096]{2,1,0:T(2,128)(2,1)}), bf16[128,1,4096]{2,1,0:T(2,128)(2,1)}) %all-gather.12.cloned.1.call-update) | async-done | bytes 1048592 | tf_op jit(solution)/shard_map/all_gather | solution.py:92
  79.3 0.8 dynamic-slice_reduce_fusion
  80.0 1.6 convert_reduce_fusion.1
  81.7 1.6 fusion.16
  83.3 46.8 %all-gather.8.cloned.1.call-done = bf16[1024,2048]{1,0:T(8,128)(2,1)} async-done(((bf16[64,2048]{1,0:T(8,128)(2,1)}), bf16[1024,2048]{1,0:T(8,128)(2,1)}) %all-gather.8.cloned.1.call-update) | async-done | bytes 4194320 | tf_op jit(solution)/shard_map/all_gather | solution.py:64
  130.1 4.7 fusion.33
  134.8 3.9 copy.59
  138.7 3.9 copy.60
  142.7 3.2 fusion.1
  145.9 0.0 copy-start.2
  145.9 2.2 convert_reduce_fusion
  148.1 0.0 copy-done.2
  148.1 2.9 fusion.14
  150.9 0.4 copy.47
  151.3 0.4 convert_element_type.63
  151.7 0.9 maximum_bitcast_fusion
  152.6 0.0 all-gather.14.cloned.1.call-update
  152.6 75.6 %all-gather.14.cloned.1.call-done = bf16[16,65,4096]{2,1,0:T(8,128)(2,1)} async-done(((bf16[1,65,4096]{2,1,0:T(8,128)(2,1)}), bf16[16,65,4096]{2,1,0:T(8,128)(2,1)}) %all-gather.14.cloned.1.call-update) | async-done | bytes 8519696 | tf_op jit(solution)/shard_map/all_gather | solution.py:27
  228.2 0.0 copy-done
  228.2 5.2 %fusion.9 = f32[16,65,256]{2,1,0:T(8,128)S(1)} fusion(bf16[16,65,4096]{2,1,0:T(8,128)(2,1)} %all-gather.14.cloned.1.call-done, bf16[4096,256]{1,0:T(8,128)(2,1)S(1)} %copy-done), kind=kOutput, calls=%fused_computation.15 | convolution fusion | flops 2181038080 | bytes 11681792 | tf_op jit(solution)/shard_map/vmap()/dot_general | solution.py:113
  233.4 0.0 copy-start.3
  233.4 0.2 reshape.68
  233.6 1.3 fusion.17
  234.9 0.7 broadcast_in_dim.47
  235.6 5.0 %all-to-all-start = ((f32[16,1,1040]{2,1,0:T(1,128)}), f32[16,1,1040]{2,1,0:T(1,128)S(1)}, u32[]{:S(2)}, u32[]{:S(2)}) async-start(f32[16,1,1040]{2,1,0:T(1,128)} %broadcast_in_dim.47), calls=%async_computation | async-start | bytes 147456 | tf_op jit(solution)/shard_map/all_to_all | solution.py:33
  240.6 0.0 all-gather.10.cloned.1.call-start
  240.6 0.0 copy-done.3
  240.6 6.4 %all-to-all-done = f32[16,1,1040]{2,1,0:T(1,128)S(1)} async-done(((f32[16,1,1040]{2,1,0:T(1,128)}), f32[16,1,1040]{2,1,0:T(1,128)S(1)}, u32[]{:S(2)}, u32[]{:S(2)}) %all-to-all-start) | async-done | bytes 66592 | tf_op jit(solution)/shard_map/all_to_all | solution.py:33
  247.1 0.1 reduce_sum.42
  247.2 2.1 fusion.8
  249.3 0.0 all-gather.10.cloned.1.call-update
  249.3 0.2 reduce-scatter.2.cloned.1.call-start
  249.5 77.3 %all-gather.10.cloned.1.call-done = bf16[1040,4096]{1,0:T(8,128)(2,1)} async-done(((bf16[1040,256]{1,0:T(8,128)(2,1)}), bf16[1040,4096]{1,0:T(8,128)(2,1)}) %all-gather.10.cloned.1.call-update) | async-done | bytes 8519696 | tf_op jit(solution)/shard_map/all_gather | solution.py:128
  326.9 12.2 %fusion.34 = f32[1040,768]{1,0:T(8,128)} fusion(bf16[1040,4096]{1,0:T(8,128)(2,1)} %all-gather.10.cloned.1.call-done, bf16[4096,768]{1,0:T(8,128)(2,1)} %param.25), kind=kOutput, calls=%fused_computation.62 | convolution fusion | flops 6543114240 | bytes 18006016 | tf_op jit(solution)/shard_map/dot_general | solution.py:129
  339.1 26.3 %fusion = bf16[4096,1040]{0,1:T(8,128)(2,1)} fusion(bf16[768,4096]{1,0:T(8,128)(2,1)} %param.27, bf16[1040,4096]{1,0:T(8,128)(2,1)} %all-gather.10.cloned.1.call-done, bf16[4096,768]{1,0:T(8,128)(2,1)} %param.26, f32[1040,768]{1,0:T(8,128)} %fusion.34), kind=kOutput, calls=%fused_computation.1 | convolution fusion | flops 13095280640 | bytes 32817152 | tf_op jit(solution)/shard_map/dot_general | solution.py:133
  365.4 0.0 copy-start.1
  365.4 0.0 reduce-scatter.2.cloned.1.call-update
  365.4 94.5 %reduce-scatter.2.cloned.1.call-done = bf16[256,1040]{0,1:T(8,128)(2,1)} async-done(((bf16[4096,1040]{0,1:T(8,128)(2,1)}), bf16[256,1040]{0,1:T(8,128)(2,1)}) %reduce-scatter.2.cloned.1.call-update) | async-done | bytes 532496 | tf_op jit(solution)/shard_map/reduce_scatter | solution.py:132
  460.0 2.0 fusion.18
  461.9 0.0 copy-done.1
  (7 shorter events, 0.1 us)
Async XLA Ops:
  6.5 221.7 %copy-start = (bf16[4096,256]{1,0:T(8,128)(2,1)S(1)}, bf16[4096,256]{1,0:T(8,128)(2,1)}, u32[]{:S(2)}) copy-start(bf16[4096,256]{1,0:T(8,128)(2,1)} %param.22) | copy-start | bytes 6291460
  6.5 10.8 %copy-start.4 = (s32[1,1024]{1,0:T(1,128)S(1)}, s32[1,1024]{1,0:T(1,128)}, u32[]{:S(2)}) copy-start(s32[1,1024]{1,0:T(1,128)} %param.16) | copy-start | bytes 12292
  6.5 72.7 %all-gather.12.cloned.1.call-start = ((), (), s32[]{:S(2)}) async-start(), calls=%async_computation.5 | async-start | bytes 2113536 | tf_op jit(solution)/shard_map/all_gather | solution.py:92
  7.3 122.8 %all-gather.8.cloned.1.call-start = ((), (), s32[]{:S(2)}) async-start(), calls=%async_computation.2 | async-start | bytes 4456448 | tf_op jit(solution)/shard_map/all_gather | solution.py:64
  8.0 220.2 %all-gather.14.cloned.1.call-start = ((), (), s32[]{:S(2)}) async-start(), calls=%async_computation.6 | async-start | bytes 10027008 | tf_op jit(solution)/shard_map/all_gather | solution.py:27
  145.9 2.2 copy-start.2
  233.4 7.2 %copy-start.3 = (s32[1,1040]{1,0:T(1,128)S(1)}, s32[1,1040]{1,0:T(1,128)}, u32[]{:S(2)}) copy-start(s32[1,1040]{1,0:T(1,128)} %param.23) | copy-start | bytes 12484
  235.6 11.5 %all-to-all-start = ((f32[16,1,1040]{2,1,0:T(1,128)}), f32[16,1,1040]{2,1,0:T(1,128)S(1)}, u32[]{:S(2)}, u32[]{:S(2)}) async-start(f32[16,1,1040]{2,1,0:T(1,128)} %broadcast_in_dim.47), calls=%async_computation | async-start | bytes 147456 | tf_op jit(solution)/shard_map/all_to_all | solution.py:33
  240.6 86.3 %all-gather.10.cloned.1.call-start = ((), (), s32[]{:S(2)}) async-start(), calls=%async_computation.3 | async-start | bytes 9052160 | tf_op jit(solution)/shard_map/all_gather | solution.py:128
  249.3 210.6 %reduce-scatter.2.cloned.1.call-start = ((), (), s32[]{:S(2)}) async-start(), calls=%async_computation.4 | async-start | bytes 9052160 | tf_op jit(solution)/shard_map/reduce_scatter | solution.py:132
  365.4 96.5 %copy-start.1 = (bf16[4096,256]{1,0:T(8,128)(2,1)S(1)}, bf16[4096,256]{1,0:T(8,128)(2,1)}, u32[]{:S(2)}) copy-start(bf16[4096,256]{1,0:T(8,128)(2,1)} %param.22) | copy-start | bytes 6291460
Sparse Core Ops, SparseCore 0:
  10.3 68.8 all-gather.11
  81.4 48.6 all-gather.7
  152.7 75.4 all-gather.13
  249.4 77.3 all-gather.9
  365.5 94.3 reduce-scatter.1
where the time goes:
time: 469 us; the launch traced here: 468 us
  waiting for transfers between devices  364 us (78%)
  matrix products  55.1 us (12%)
  local copies, waits for them, and re-layouts  21.7 us (5%)
  between operations  15.9 us (3%)
  other arithmetic  6.54 us (1%)
  starting transfers between devices  5.32 us (1%)
    reduce_scatter x1, waiting for transfers between devices, shards(): lax.psum_scatter(lax.dot_general(w_down, hidden, (((0,), (1,)), ((), ()))...  94.5 us
    all_gather x1, waiting for transfers between devices, shards(): piece = lax.all_gather(normed_part, 'tok', axis=1, tiled=True)  77.3 us
    all_gather x1, waiting for transfers between devices, piecewise(): gathered.append(jax.vmap(apply)(lax.all_gather(share, axis), starts))  75.6 us
    all_gather x1, waiting for transfers between devices, shards(): all_queries = lax.all_gather(dec_q, ('grp', 'tok'), axis=0, tiled=True)  61.7 us
    all_gather x1, waiting for transfers between devices, shards(): piece = lax.all_gather(pre_kv, 'tok', axis=0, tiled=True)  46.8 us
    dot_general x1, matrix products, shards(): lax.dot_general(w_down, hidden, (((0,), (1,)), ((), ())), preferred_eleme...  26.3 us
    dot_general x1, matrix products, shards(): gate_part = jnp.dot(piece, w_gate, preferred_element_type=jnp.float32)  12.2 us
    unnamed x13, local copies, waits for them, and re-layouts  11.9 us
  transfers between devices with their start and end apart: 6, of which 6 were waited for; matrix products, arithmetic and copies ran while one was open for 2% of the time, Pallas kernels for 0%

commit v1 on v0

--- a/solution.py
+++ b/solution.py
@@ -89,7 +89,10 @@
         .reshape(local_rows, D)
         .astype(jnp.bfloat16)
     )
-    all_queries = lax.all_gather(dec_q, ("grp", "tok"), axis=0, tiled=True)
+    all_queries = jnp.concatenate(
+        lax.all_to_all(jnp.stack([dec_q] * lax.axis_size(("grp", "tok"))), ("grp", "tok"), 0, 0),
+        axis=0,
+    )
     slot = lax.axis_index(("grp", "tok"))
     request = slot_request[slot]
     query_row = lax.dynamic_slice_in_dim(all_queries, request, 1, 0).reshape(KVH, group, HD)

time: 469 us -> 409 us (0.87)
  waiting for transfers between devices: 364 us -> 273 us
  starting transfers between devices: 5.32 us -> 17 us
  local copies, waits for them, and re-layouts: 21.7 us -> 31 us
  other arithmetic: 6.54 us -> 15.7 us
    all_gather x1 -> x0, waiting for transfers between devices: 61.7 us -> none  [shards(): all_queries = lax.all_gather(dec_q, ('grp', 'tok'), axis=0, tiled=True)]
    all_gather x1, waiting for transfers between devices: 46.8 us -> 9.31 us  [shards(): piece = lax.all_gather(pre_kv, 'tok', axis=0, tiled=True)]
    all_to_all x0 -> x1, starting transfers between devices: none -> 11.5 us  [shards(): lax.all_to_all(jnp.stack([dec_q] * lax.axis_size(('grp', 'tok'))), ('grp'...]
    all_to_all x0 -> x1, waiting for transfers between devices: none -> 9.27 us  [shards(): lax.all_to_all(jnp.stack([dec_q] * lax.axis_size(('grp', 'tok'))), ('grp'...]
    another operation x0 -> x1, other arithmetic: none -> 8.39 us  [shards(): jnp.stack([dec_q] * lax.axis_size(('grp', 'tok')))]
    unnamed x13 -> x19, local copies, waits for them, and re-layouts: 11.9 us -> 17 us
  transfers between devices with their start and end apart: 6 -> 6, of which waited for: 6 -> 6; matrix products, arithmetic and copies ran while one was open for 2% -> 7% of each run, Pallas kernels for 0% -> 0%
where the time goes in v1:
time: 409 us; the launch traced here: 408 us
  waiting for transfers between devices  273 us (67%)
  matrix products  55.2 us (13%)
  local copies, waits for them, and re-layouts  31 us (8%)
  starting transfers between devices  17 us (4%)
  between operations  16 us (4%)
  other arithmetic  15.7 us (4%)
    reduce_scatter x1, waiting for transfers between devices, shards(): lax.psum_scatter(lax.dot_general(w_down, hidden, (((0,), (1,)), ((), ()))...  94.6 us
    all_gather x1, waiting for transfers between devices, shards(): piece = lax.all_gather(normed_part, 'tok', axis=1, tiled=True)  77.3 us
    all_gather x1, waiting for transfers between devices, piecewise(): gathered.append(jax.vmap(apply)(lax.all_gather(share, axis), starts))  75.1 us
    dot_general x1, matrix products, shards(): lax.dot_general(w_down, hidden, (((0,), (1,)), ((), ())), preferred_eleme...  26.4 us
    unnamed x19, local copies, waits for them, and re-layouts  17 us
    dot_general x1, matrix products, shards(): gate_part = jnp.dot(piece, w_gate, preferred_element_type=jnp.float32)  12.2 us
    all_to_all x1, starting transfers between devices, shards(): lax.all_to_all(jnp.stack([dec_q] * lax.axis_size(('grp', 'tok'))), ('grp'...  11.5 us
    all_gather x1, waiting for transfers between devices, shards(): piece = lax.all_gather(pre_kv, 'tok', axis=0, tiled=True)  9.31 us
  transfers between devices with their start and end apart: 6, of which 6 were waited for; matrix products, arithmetic and copies ran while one was open for 7% of the time, Pallas kernels for 0%

profile of v1, /device:TPU:1, one launch (start us, length us, event | category | flops | bytes accessed | tf_op | source)
XLA Modules:
  0.0 407.7 jit_solution(12820647299322338144)
XLA Ops:
  6.5 0.0 copy-start
  6.5 0.0 all-gather.6.cloned.1.call-start
  6.5 0.7 all-gather.6.cloned.1.call-update
  7.3 0.8 reduce.1
  8.0 3.4 stack.2
  11.4 0.5 broadcast.59
  12.0 0.0 copy-start.6
  12.0 8.4 %reduce.5 = bf16[128,4096]{1,0:T(8,128)(2,1)S(1)} reduce(bf16[128,1,4096]{2,1,0:T(2,128)(2,1)} %stack.2, bf16[]{:T(256)} %broadcast.59), dimensions={1}, to_apply=%stack.2.reduce_sub_computation | reduce | bytes 2097154 | tf_op jit(solution)/shard_map/stack | solution.py:93
  20.4 1.6 reshape.85
  22.0 0.0 copy-start.5
  22.0 11.5 %all-to-all-start = ((bf16[128,2,2048]{2,1,0:T(2,128)(2,1)}), bf16[128,2,2048]{2,1,0:T(2,128)(2,1)S(1)}, u32[]{:S(2)}, u32[]{:S(2)}) async-start(bf16[128,2,2048]{2,1,0:T(2,128)(2,1)} %reshape.85), calls=%async_computation | async-start | bytes 2097152 | tf_op jit(solution)/shard_map/all_to_all | solution.py:93
  33.5 0.2 all-gather.10.cloned.1.call-start
  33.7 0.0 copy-done.6
  33.7 0.7 dynamic_slice.13
  36.4 2.2 reshape.71
  38.6 3.9 copy.48
  43.3 0.0 copy-done.5
  43.3 0.1 fusion.29
  43.4 0.1 fusion.22
  43.5 9.3 %all-to-all-done = bf16[128,2,2048]{2,1,0:T(2,128)(2,1)S(1)} async-done(((bf16[128,2,2048]{2,1,0:T(2,128)(2,1)}), bf16[128,2,2048]{2,1,0:T(2,128)(2,1)S(1)}, u32[]{:S(2)}, u32[]{:S(2)}) %all-to-all-start) | async-done | bytes 1048608 | tf_op jit(solution)/shard_map/all_to_all | solution.py:93
  52.8 3.5 reshape.86
  56.2 0.8 dynamic-slice_reduce_fusion
  57.0 1.7 convert_reduce_fusion.1
  58.7 1.6 fusion.16
  60.4 9.3 %all-gather.6.cloned.1.call-done = bf16[1024,2048]{1,0:T(8,128)(2,1)} async-done(((bf16[64,2048]{1,0:T(8,128)(2,1)}), bf16[1024,2048]{1,0:T(8,128)(2,1)}) %all-gather.6.cloned.1.call-update) | async-done | bytes 4194320 | tf_op jit(solution)/shard_map/all_gather | solution.py:64
  69.7 4.6 %fusion.33 = (bf16[1024,1024]{1,0:T(8,128)(2,1)}, bf16[1024,1024]{1,0:T(8,128)(2,1)}) fusion(bf16[1024,2048]{1,0:T(8,128)(2,1)} %all-gather.6.cloned.1.call-done), kind=kLoop, calls=%fused_computation.61 | loop fusion | bytes 8388608 | tf_op jit(solution)/shard_map/slice | solution.py:69
  74.3 0.0 copy-start.3
  74.3 4.0 copy.59
  78.3 4.0 copy.60
  82.3 0.0 copy-done.3
  82.3 3.2 fusion.1
  85.5 0.0 copy-start.2
  85.5 2.2 convert_reduce_fusion
  87.7 0.0 copy-done.2
  87.7 2.9 fusion.14
  90.5 0.4 copy.47
  91.0 0.4 convert_element_type.63
  91.4 0.9 maximum_bitcast_fusion
  92.2 0.0 all-gather.10.cloned.1.call-update
  92.2 75.1 %all-gather.10.cloned.1.call-done = bf16[16,65,4096]{2,1,0:T(8,128)(2,1)} async-done(((bf16[1,65,4096]{2,1,0:T(8,128)(2,1)}), bf16[16,65,4096]{2,1,0:T(8,128)(2,1)}) %all-gather.10.cloned.1.call-update) | async-done | bytes 8519696 | tf_op jit(solution)/shard_map/all_gather | solution.py:27
  167.3 0.0 copy-done
  167.3 5.2 %fusion.9 = f32[16,65,256]{2,1,0:T(8,128)S(1)} fusion(bf16[16,65,4096]{2,1,0:T(8,128)(2,1)} %all-gather.10.cloned.1.call-done, bf16[4096,256]{1,0:T(8,128)(2,1)S(1)} %copy-done), kind=kOutput, calls=%fused_computation.15 | convolution fusion | flops 2181038080 | bytes 11681792 | tf_op jit(solution)/shard_map/vmap()/dot_general | solution.py:116
  172.5 0.0 copy-start.4
  172.5 0.2 reshape.74
  172.7 1.3 fusion.17
  174.0 0.7 broadcast_in_dim.47
  174.7 5.0 %all-to-all-start.1 = ((f32[16,1,1040]{2,1,0:T(1,128)}), f32[16,1,1040]{2,1,0:T(1,128)S(1)}, u32[]{:S(2)}, u32[]{:S(2)}) async-start(f32[16,1,1040]{2,1,0:T(1,128)} %broadcast_in_dim.47), calls=%async_computation.1 | async-start | bytes 147456 | tf_op jit(solution)/shard_map/all_to_all | solution.py:33
  179.7 0.0 all-gather.8.cloned.1.call-start
  179.7 0.0 copy-done.4
  179.8 6.4 %all-to-all-done.1 = f32[16,1,1040]{2,1,0:T(1,128)S(1)} async-done(((f32[16,1,1040]{2,1,0:T(1,128)}), f32[16,1,1040]{2,1,0:T(1,128)S(1)}, u32[]{:S(2)}, u32[]{:S(2)}) %all-to-all-start.1) | async-done | bytes 66592 | tf_op jit(solution)/shard_map/all_to_all | solution.py:33
  186.2 0.1 reduce_sum.42
  186.3 2.1 fusion.8
  188.4 0.0 all-gather.8.cloned.1.call-update
  188.4 0.3 reduce-scatter.2.cloned.1.call-start
  188.7 77.3 %all-gather.8.cloned.1.call-done = bf16[1040,4096]{1,0:T(8,128)(2,1)} async-done(((bf16[1040,256]{1,0:T(8,128)(2,1)}), bf16[1040,4096]{1,0:T(8,128)(2,1)}) %all-gather.8.cloned.1.call-update) | async-done | bytes 8519696 | tf_op jit(solution)/shard_map/all_gather | solution.py:131
  266.0 12.2 %fusion.34 = f32[1040,768]{1,0:T(8,128)} fusion(bf16[1040,4096]{1,0:T(8,128)(2,1)} %all-gather.8.cloned.1.call-done, bf16[4096,768]{1,0:T(8,128)(2,1)} %param.25), kind=kOutput, calls=%fused_computation.62 | convolution fusion | flops 6543114240 | bytes 18006016 | tf_op jit(solution)/shard_map/dot_general | solution.py:132
  278.2 26.4 %fusion = bf16[4096,1040]{0,1:T(8,128)(2,1)} fusion(bf16[768,4096]{1,0:T(8,128)(2,1)} %param.27, bf16[1040,4096]{1,0:T(8,128)(2,1)} %all-gather.8.cloned.1.call-done, bf16[4096,768]{1,0:T(8,128)(2,1)} %param.26, f32[1040,768]{1,0:T(8,128)} %fusion.34), kind=kOutput, calls=%fused_computation.1 | convolution fusion | flops 13095280640 | bytes 32817152 | tf_op jit(solution)/shard_map/dot_general | solution.py:136
  304.5 0.0 copy-start.1
  304.5 0.0 reduce-scatter.2.cloned.1.call-update
  304.5 94.6 %reduce-scatter.2.cloned.1.call-done = bf16[256,1040]{0,1:T(8,128)(2,1)} async-done(((bf16[4096,1040]{0,1:T(8,128)(2,1)}), bf16[256,1040]{0,1:T(8,128)(2,1)}) %reduce-scatter.2.cloned.1.call-update) | async-done | bytes 532496 | tf_op jit(solution)/shard_map/reduce_scatter | solution.py:135
  399.2 2.0 fusion.18
  401.1 0.0 copy-done.1
  (7 shorter events, 0.1 us)
Async XLA Ops:
  6.5 160.8 %copy-start = (bf16[4096,256]{1,0:T(8,128)(2,1)S(1)}, bf16[4096,256]{1,0:T(8,128)(2,1)}, u32[]{:S(2)}) copy-start(bf16[4096,256]{1,0:T(8,128)(2,1)} %param.22) | copy-start | bytes 6291460
  6.5 63.1 %all-gather.6.cloned.1.call-start = ((), (), s32[]{:S(2)}) async-start(), calls=%async_computation.3 | async-start | bytes 4456448 | tf_op jit(solution)/shard_map/all_gather | solution.py:64
  12.0 21.8 %copy-start.6 = (s32[128]{0:T(128)S(1)}, s32[128]{0:T(128)}, u32[]{:S(2)}) copy-start(s32[128]{0:T(128)} %param.20) | copy-start | bytes 1540
  22.0 21.3 %copy-start.5 = (s32[1,1024]{1,0:T(1,128)S(1)}, s32[1,1024]{1,0:T(1,128)}, u32[]{:S(2)}) copy-start(s32[1,1024]{1,0:T(1,128)} %param.16) | copy-start | bytes 12292
  22.0 30.8 %all-to-all-start = ((bf16[128,2,2048]{2,1,0:T(2,128)(2,1)}), bf16[128,2,2048]{2,1,0:T(2,128)(2,1)S(1)}, u32[]{:S(2)}, u32[]{:S(2)}) async-start(bf16[128,2,2048]{2,1,0:T(2,128)(2,1)} %reshape.85), calls=%async_computation | async-start | bytes 2097152 | tf_op jit(solution)/shard_map/all_to_all | solution.py:93
  33.5 133.8 %all-gather.10.cloned.1.call-start = ((), (), s32[]{:S(2)}) async-start(), calls=%async_computation.6 | async-start | bytes 10027008 | tf_op jit(solution)/shard_map/all_gather | solution.py:27
  74.3 8.0 %copy-start.3 = (bf16[64,8,4,128]{3,2,1,0:T(4,128)(2,1)S(1)}, bf16[64,8,4,128]{3,2,1,0:T(4,128)(2,1)}, u32[]{:S(2)}) copy-start(bf16[64,8,4,128]{3,2,1,0:T(4,128)(2,1)} %reshape.71) | copy-start | bytes 1572868
  85.5 2.2 copy-start.2
  172.5 7.2 %copy-start.4 = (s32[1,1040]{1,0:T(1,128)S(1)}, s32[1,1040]{1,0:T(1,128)}, u32[]{:S(2)}) copy-start(s32[1,1040]{1,0:T(1,128)} %param.23) | copy-start | bytes 12484
  174.7 11.5 %all-to-all-start.1 = ((f32[16,1,1040]{2,1,0:T(1,128)}), f32[16,1,1040]{2,1,0:T(1,128)S(1)}, u32[]{:S(2)}, u32[]{:S(2)}) async-start(f32[16,1,1040]{2,1,0:T(1,128)} %broadcast_in_dim.47), calls=%async_computation.1 | async-start | bytes 147456 | tf_op jit(solution)/shard_map/all_to_all | solution.py:33
  179.7 86.3 %all-gather.8.cloned.1.call-start = ((), (), s32[]{:S(2)}) async-start(), calls=%async_computation.4 | async-start | bytes 9052160 | tf_op jit(solution)/shard_map/all_gather | solution.py:131
  188.4 210.7 %reduce-scatter.2.cloned.1.call-start = ((), (), s32[]{:S(2)}) async-start(), calls=%async_computation.5 | async-start | bytes 9052160 | tf_op jit(solution)/shard_map/reduce_scatter | solution.py:135
  304.5 96.6 %copy-start.1 = (bf16[4096,256]{1,0:T(8,128)(2,1)S(1)}, bf16[4096,256]{1,0:T(8,128)(2,1)}, u32[]{:S(2)}) copy-start(bf16[4096,256]{1,0:T(8,128)(2,1)} %param.22) | copy-start | bytes 6291460
Sparse Core Ops, SparseCore 0:
  9.5 60.1 all-gather.5
  92.4 74.9 all-gather.9
  188.5 77.3 all-gather.7
  304.7 94.4 reduce-scatter.1
